TPU v7x, 32 devices: a whole 2x2x4 slice. The times are simulated.
32 devices in a mesh: nodes: 16 (over z, y, x), rep: 2 (over core).
Axes of the slice: x: 2, y: 2, z: 4, core: 2. Of those that a mesh axis runs over, the one named last changes fastest.
Arguments:
- node_latent: bfloat16 [5120, 512], P(('nodes', 'rep')), may hold values from -6 to 6
- edge_saved: bfloat16 [40960, 512], P(('nodes', 'rep')), may hold values from -6 to 6
- node_cot: bfloat16 [5120, 512], P(('nodes', 'rep')), may hold values from -6 to 6
- edge_cot: bfloat16 [40960, 512], P(('nodes', 'rep')), may hold values from -6 to 6
- senders: int32 [40960], P(('nodes', 'rep')), may hold values from 0 to 447, as said below
- receivers: int32 [40960], P(('nodes', 'rep')), may hold values from 0 to 319
- ghost_rows: int32 [16, 16, 8], P('nodes'), may hold values from 0 to 319, as said below
- w_edge_in: bfloat16 [1536, 512], replicated, may hold values from -0.15625 to 0.15625
- w_edge_out: bfloat16 [512, 512], replicated, may hold values from -0.25 to 0.25
- edge_gain: float32 [512], replicated, may hold values from 0.5 to 2
- edge_offset: float32 [512], replicated, may hold values from -3 to 3
- w_node_in: bfloat16 [1024, 512], replicated, may hold values from -0.1875 to 0.1875
- w_node_out: bfloat16 [512, 512], replicated, may hold values from -0.25 to 0.25
- node_gain: float32 [512], replicated, may hold values from 0.5 to 2
Outputs:
- grad_nodes: bfloat16 [5120, 512], P(('nodes', 'rep'))
- grad_edges: bfloat16 [40960, 512], P(('nodes', 'rep'))
- grad_edge_in: bfloat16 [1536, 512], replicated
- grad_edge_out: bfloat16 [512, 512], replicated
- grad_node_in: bfloat16 [1024, 512], replicated
- grad_node_out: bfloat16 [512, 512], replicated
Inputs may be any that keep to these rules, and one draw needn't show every extreme that they name: `senders`: A sender below 320 is a node of the edge's own partition; otherwise it is 320 + q * 8 + s, the ghost slot s of the list of a partition q other than the edge's own. Each list ghost_rows[q, p] holds 8 distinct rows.
All inputs are finite; a program needn't handle non-finite values.
Results may differ from a plain program's by a relative error of at most 0.008.
Values may be sent and summed in bfloat16 or wider, within the bound.
A program may use at most 128 MiB of HBM per device.

v0:
```python
import math

import jax
import jax.numpy as jnp
from jax import lax
from jax.sharding import PartitionSpec as P

EPS = 1e-05


def swapped(array, axis, bit):
    return lax.ppermute(array, axis, [(i, i ^ 1 << bit) for i in range(lax.axis_size(axis))])


def mat_mul(left, right):
    return jnp.dot(left, right, preferred_element_type=jnp.float32)


def mat_tn(left, right):
    return lax.dot_general(
        left, right, (((0,), (0,)), ((), ())), preferred_element_type=jnp.float32
    )


def mat_nt(left, right):
    return lax.dot_general(
        left, right, (((1,), (1,)), ((), ())), preferred_element_type=jnp.float32
    )


def silu_slope(value):
    sigmoid_v = jax.nn.sigmoid(value)
    return sigmoid_v * (1.0 + value * (1.0 - sigmoid_v))


def norm_forward(value):
    centred = value - jnp.mean(value, axis=-1, keepdims=True)
    inverse = lax.rsqrt(jnp.mean(centred * centred, axis=-1, keepdims=True) + EPS)
    return (centred * inverse, inverse)


def norm_backward(grad_hat, normed, inverse):
    return inverse * (
        grad_hat
        - jnp.mean(grad_hat, axis=-1, keepdims=True)
        - normed * jnp.mean(grad_hat * normed, axis=-1, keepdims=True)
    )


def edge_forward(edge_block, send_rows, recv_rows, w_edge_in, w_edge_out, edge_gain, edge_offset):
    latent_width = edge_block.shape[1]
    pre_act = (
        mat_mul(edge_block, w_edge_in[:latent_width])
        + mat_mul(send_rows, w_edge_in[latent_width : 2 * latent_width])
        + mat_mul(recv_rows, w_edge_in[2 * latent_width :])
    )
    edge_hidden = jax.nn.silu(pre_act).astype(jnp.bfloat16)
    edge_normed, edge_inverse = norm_forward(mat_mul(edge_hidden, w_edge_out))
    message = edge_normed * edge_gain + edge_offset
    return (pre_act, edge_hidden, edge_normed, edge_inverse, message)


def edge_backward(
    edge_block,
    send_rows,
    recv_rows,
    edge_cot,
    message_grad,
    saved,
    w_edge_in,
    w_edge_out,
    edge_gain,
):
    pre_act, edge_hidden, edge_normed, edge_inverse = saved
    latent_width = edge_block.shape[1]
    grad_out = norm_backward(message_grad * edge_gain, edge_normed, edge_inverse).astype(
        jnp.bfloat16
    )
    grad_act = (mat_nt(grad_out, w_edge_out) * silu_slope(pre_act)).astype(jnp.bfloat16)
    in_grad = jnp.concatenate(
        [mat_tn(edge_block, grad_act), mat_tn(send_rows, grad_act), mat_tn(recv_rows, grad_act)], 0
    )
    out_grad = mat_tn(edge_hidden, grad_out)
    edge_grad = (edge_cot.astype(jnp.float32) + mat_nt(grad_act, w_edge_in[:latent_width])).astype(
        jnp.bfloat16
    )
    send_grad = mat_nt(grad_act, w_edge_in[latent_width : 2 * latent_width])
    recv_grad = mat_nt(grad_act, w_edge_in[2 * latent_width :])
    return (edge_grad, send_grad, recv_grad, in_grad, out_grad)


def node_pass(node_rows, totals_b, node_cot, w_node_in, w_node_out, node_gain):
    latent_width = node_rows.shape[1]
    node_pre = mat_mul(node_rows, w_node_in[:latent_width]) + mat_mul(
        totals_b, w_node_in[latent_width:]
    )
    node_hidden = jax.nn.silu(node_pre).astype(jnp.bfloat16)
    node_normed, node_inverse = norm_forward(mat_mul(node_hidden, w_node_out))
    grad_out = norm_backward(
        node_cot.astype(jnp.float32) * node_gain, node_normed, node_inverse
    ).astype(jnp.bfloat16)
    grad_act = (mat_nt(grad_out, w_node_out) * silu_slope(node_pre)).astype(jnp.bfloat16)
    in_grad = jnp.concatenate([mat_tn(node_rows, grad_act), mat_tn(totals_b, grad_act)], 0)
    direct_grad = mat_nt(grad_act, w_node_in[:latent_width])
    totals_grad = mat_nt(grad_act, w_node_in[latent_width:]).astype(jnp.bfloat16)
    return (direct_grad, totals_grad, in_grad, mat_tn(node_hidden, grad_out))


def shards(
    node_latent,
    edge_saved,
    node_cot,
    edge_cot,
    senders,
    receivers,
    ghost_rows,
    w_edge_in,
    w_edge_out,
    edge_gain,
    edge_offset,
    w_node_in,
    w_node_out,
    node_gain,
):
    latent_width = node_latent.shape[1]
    edge_latent = swapped(edge_saved, "rep", 0)
    partition = lax.all_gather(node_latent, "rep", axis=0, tiled=True)
    part_rows = partition.shape[0]
    ghost_lists = ghost_rows[0]
    part_count = ghost_lists.shape[0]
    slot_count = ghost_lists.shape[1]
    outgoing = partition[ghost_lists.reshape(-1)].reshape(part_count, slot_count, latent_width)
    ghosts = lax.all_to_all(outgoing, "nodes", split_axis=0, concat_axis=0, tiled=True)
    node_table = jnp.concatenate(
        [partition, ghosts.reshape(part_count * slot_count, latent_width)], 0
    )
    send_rows = node_table[senders]
    recv_rows = partition[receivers]
    pre_act, edge_hidden, edge_normed, edge_inverse, message = edge_forward(
        edge_latent, send_rows, recv_rows, w_edge_in, w_edge_out, edge_gain, edge_offset
    )
    partial_totals = jax.ops.segment_sum(message, receivers, num_segments=part_rows)
    totals = lax.psum_scatter(partial_totals, "rep", scatter_dimension=0, tiled=True)
    direct_grad, totals_grad, node_in_grad, node_out_grad = node_pass(
        node_latent, totals.astype(jnp.bfloat16), node_cot, w_node_in, w_node_out, node_gain
    )
    partition_totals_grad = lax.all_gather(totals_grad, "rep", axis=0, tiled=True)
    message_grad = edge_cot.astype(jnp.float32) + partition_totals_grad[receivers].astype(
        jnp.float32
    )
    edge_grad, send_grad, recv_grad, edge_in_grad, edge_out_grad = edge_backward(
        edge_latent,
        send_rows,
        recv_rows,
        edge_cot,
        message_grad,
        (pre_act, edge_hidden, edge_normed, edge_inverse),
        w_edge_in,
        w_edge_out,
        edge_gain,
    )
    table_grad = jax.ops.segment_sum(send_grad, senders, num_segments=node_table.shape[0])
    row_grad = table_grad[:part_rows] + jax.ops.segment_sum(
        recv_grad, receivers, num_segments=part_rows
    )
    ghost_grad = table_grad[part_rows:].reshape(part_count, slot_count, latent_width)
    returned = lax.all_to_all(
        ghost_grad.astype(jnp.bfloat16), "nodes", split_axis=0, concat_axis=0, tiled=True
    ).astype(ghost_grad.dtype)
    row_grad = row_grad + jax.ops.segment_sum(
        returned.reshape(-1, latent_width), ghost_lists.reshape(-1), num_segments=part_rows
    )
    own_grad = lax.psum_scatter(row_grad, "rep", scatter_dimension=0, tiled=True)
    grad_nodes = (own_grad + direct_grad + node_cot.astype(jnp.float32)).astype(jnp.bfloat16)
    weight_grads = (edge_in_grad, edge_out_grad, node_in_grad, node_out_grad)
    device_count = lax.axis_size("nodes") * lax.axis_size("rep")
    edge_scale = 1.0 / math.sqrt(senders.shape[0] * device_count)
    node_scale = 1.0 / math.sqrt(node_latent.shape[0] * device_count)
    weight_total = lax.psum(
        (weight_grads[0], weight_grads[1], weight_grads[2], weight_grads[3]), ("nodes", "rep")
    )
    return (
        grad_nodes,
        edge_grad,
        (weight_total[0] * edge_scale).astype(jnp.bfloat16),
        (weight_total[1] * edge_scale).astype(jnp.bfloat16),
        (weight_total[2] * node_scale).astype(jnp.bfloat16),
        (weight_total[3] * node_scale).astype(jnp.bfloat16),
    )


def solution(mesh):
    return jax.shard_map(
        shards,
        mesh=mesh,
        in_specs=(
            P(("nodes", "rep"), None),
            P(("nodes", "rep"), None),
            P(("nodes", "rep"), None),
            P(("nodes", "rep"), None),
            P(("nodes", "rep")),
            P(("nodes", "rep")),
            P("nodes", None, None),
            P(),
            P(),
            P(),
            P(),
            P(),
            P(),
            P(),
        ),
        out_specs=(P(("nodes", "rep"), None), P(("nodes", "rep"), None), P(), P(), P(), P()),
        check_vma=False,
    )
```

profile of v0, /device:TPU:1, one launch (start us, length us, event | category | flops | bytes accessed | tf_op | source)
XLA Modules:
  0.0 328.4 jit_solution(6399339282677917739)
XLA Ops:
  7.2 2.4 all_gather.6
  11.9 7.7 %all-to-all-start = ((bf16[16,8,512]{2,1,0:T(8,128)(2,1)}), bf16[16,8,512]{2,1,0:T(8,128)(2,1)S(1)}, u32[]{:S(2)}, u32[]{:S(2)}) async-start(bf16[16,8,512]{2,1,0:T(8,128)(2,1)} %bitcast.1), calls=%async_computation | async-start | bytes 262144 | tf_op jit(solution)/shard_map/all_to_all | solution.py:133
  21.1 4.1 %gather_fusion.2 = bf16[1280,512]{1,0:T(8,128)(2,1)S(1)} fusion(bf16[320,512]{1,0:T(8,128)(2,1)S(1)} %all_gather.6, s32[2048]{0:T(1024)S(1)} %pad_clamp_fusion), kind=kCustom, calls=%fused_computation.2 | custom fusion | bytes 2626560 | tf_op jit(solution)/shard_map/gather | solution.py:138
  25.3 3.8 %fusion.15 = f32[1280,512]{1,0:T(8,128)} fusion(bf16[1280,512]{1,0:T(8,128)(2,1)S(1)} %gather_fusion.2, bf16[1536,512]{1,0:T(8,128)(2,1)} %param.21), kind=kOutput, calls=%fused_computation.46 | convolution fusion | flops 671088640 | bytes 4456448 | tf_op jit(solution)/shard_map/dot_general | solution.py:16
  29.1 4.1 %gather_fusion.1 = bf16[1280,512]{1,0:T(8,128)(2,1)S(1)} fusion(bf16[448,512]{1,0:T(8,128)(2,1)S(1)} %pad_maximum_fusion.2, s32[2048]{0:T(1024)S(1)} %pad_clamp_fusion.1), kind=kCustom, calls=%fused_computation.1 | custom fusion | bytes 2626560 | tf_op jit(solution)/shard_map/gather | solution.py:137
  33.2 2.4 fusion.19
  35.7 4.2 %multiply_convert_fusion.2 = (bf16[1280,512]{1,0:T(8,128)(2,1)S(1)}, f32[1280,512]{1,0:T(8,128)}) fusion(f32[1280,512]{1,0:T(8,128)S(1)} %copy-done.12, f32[1280,512]{1,0:T(8,128)S(1)} %fusion.19, bf16[1280,512]{1,0:T(8,128)(2,1)} %collective-permute-done, bf16[1536,512]{1,0:T(8,128)(2,1)} %param.21), kind=kOutput, calls=%fused_computation.22 | convolution fusion | flops 675676160 | bytes 11010048 | tf_op jit(solution)/shard_map/dot_general | solution.py:16
  41.7 1.9 multiply_add_fusion
  43.6 3.2 copy.28
  46.8 11.1 %scatter_custom_fusion = f32[320,512]{1,0:T(8,128)} fusion(s32[1280]{0:T(1024)S(1)} %copy-done.34, f32[1280,512]{1,0:T(8,128)} %copy.28, f32[]{:T(128)} %constant.10.clone.1), kind=kCustom, calls=%fused_computation.70 | custom fusion | flops 655360 | bytes 655872 | tf_op jit(solution)/shard_map/scatter-add | solution.py:142
  58.1 2.4 copy.27
  60.5 2.0 fusion.11
  62.5 4.8 %reduce-scatter.3.cloned.1.call-done = f32[160,512]{1,0:T(8,128)} async-done(((f32[320,512]{1,0:T(8,128)}), f32[160,512]{1,0:T(8,128)}) %reduce-scatter.3.cloned.1.call-update) | async-done | bytes 327696 | tf_op jit(solution)/shard_map/reduce_scatter | solution.py:143
  72.4 2.2 all_gather.7
  74.6 4.7 %gather_fusion.3 = bf16[1280,512]{1,0:T(8,128)(2,1)} fusion(bf16[320,512]{1,0:T(8,128)(2,1)S(1)} %all_gather.7, s32[2048]{0:T(1024)S(1)} %pad_clamp_fusion), kind=kCustom, calls=%fused_computation.3 | custom fusion | bytes 2626560 | tf_op jit(solution)/shard_map/gather | solution.py:148
  79.3 2.4 copy.29
  81.7 2.7 fusion.4
  87.7 2.4 fusion.17
  90.1 2.4 fusion.13
  92.5 10.6 %scatter_custom_fusion.1 = f32[448,512]{1,0:T(8,128)S(1)} fusion(s32[1280]{0:T(1024)S(1)} %copy-done.36, f32[1280,512]{1,0:T(8,128)} %fusion.17, f32[]{:T(128)} %constant.10.clone.1), kind=kCustom, calls=%fused_computation.55 | custom fusion | flops 655360 | bytes 918016 | tf_op jit(solution)/shard_map/scatter-add | solution.py:162
  103.8 3.2 fusion.50
  108.5 6.6 %all-to-all-start.1 = ((bf16[16,8,512]{2,1,0:T(8,128)(2,1)}), bf16[16,8,512]{2,1,0:T(8,128)(2,1)S(1)}, u32[]{:S(2)}, u32[]{:S(2)}) async-start(bf16[16,8,512]{2,1,0:T(8,128)(2,1)} %fusion.37), calls=%async_computation.2 | async-start | bytes 262144 | tf_op jit(solution)/shard_map/all_to_all | solution.py:167
  115.2 10.7 %scatter_fusion = f32[320,512]{1,0:T(8,128)S(1)} fusion(f32[320,512]{1,0:T(8,128)S(1)} %slice.42, s32[1280]{0:T(1024)S(1)} %copy-done.34, f32[1280,512]{1,0:T(8,128)} %fusion.13), kind=kCustom, calls=%fused_computation.6 | custom fusion | flops 655360 | bytes 7869440 | tf_op jit(solution)/shard_map/scatter-add | solution.py:163
  131.3 3.2 pad_maximum_fusion.1
  136.2 1.9 fusion.51
  138.1 2.3 convolution_bitcast_fusion
  140.4 2.0 pad_maximum_fusion
  143.8 3.0 fusion.1
  146.7 2.5 copy.32
  149.3 2.0 fusion.7
  151.2 163.9 %all-reduce.3.cloned.1.call-done = (f32[1536,512]{1,0:T(8,128)}, f32[512,512]{1,0:T(8,128)}, f32[1024,512]{1,0:T(8,128)}, f32[512,512]{1,0:T(8,128)}) async-done(((f32[1536,512]{1,0:T(8,128)}, f32[512,512]{1,0:T(8,128)}, f32[1024,512]{1,0:T(8,128)}, f32[512,512]{1,0:T(8,128)}), (f32[1536,512]{1,0:T(8,128)}, f32[512,512]{1,0:T(8,128)}, f32[1024,512]{1,0:T(8,128)}, ...) | async-done | bytes 7340048 | tf_op jit(solution)/shard_map/psum | solution.py:179
  315.1 3.6 %multiply_convert_fusion = bf16[1536,512]{1,0:T(8,128)(2,1)} fusion(f32[1536,512]{1,0:T(8,128)} %get-tuple-element.22), kind=kLoop, calls=%fused_computation.14 | loop fusion | flops 1572864 | bytes 4718592 | tf_op jit(solution)/shard_map/convert_element_type | solution.py:185
  (132 shorter events, 27.6 us)
Async XLA Ops:
  7.2 32.7 %copy-start = (bf16[512,512]{1,0:T(8,128)(2,1)S(1)}, bf16[512,512]{1,0:T(8,128)(2,1)}, u32[]{:S(2)}) copy-start(bf16[512,512]{1,0:T(8,128)(2,1)} %param.22) | copy-start | bytes 1572868
  11.9 17.1 %all-to-all-start = ((bf16[16,8,512]{2,1,0:T(8,128)(2,1)}), bf16[16,8,512]{2,1,0:T(8,128)(2,1)S(1)}, u32[]{:S(2)}, u32[]{:S(2)}) async-start(bf16[16,8,512]{2,1,0:T(8,128)(2,1)} %bitcast.1), calls=%async_computation | async-start | bytes 262144 | tf_op jit(solution)/shard_map/all_to_all | solution.py:133
  19.7 47.6 %reduce-scatter.3.cloned.1.call-start = ((), (), s32[]{:S(2)}) async-start(), calls=%async_computation.4 | async-start | bytes 983040 | tf_op jit(solution)/shard_map/reduce_scatter | solution.py:143
  19.7 15.9 %collective-permute-start = (bf16[1280,512]{1,0:T(8,128)(2,1)}, bf16[1280,512]{1,0:T(8,128)(2,1)}, u32[]{:S(2)}, u32[]{:S(2)}) collective-permute-start(bf16[1280,512]{1,0:T(8,128)(2,1)} %param.15), channel_id=1, source_target_pairs={{0,1},{1,0},{2,3},{3,2},{4,5},{5,4},{6,7},{7,6},{8,9},{9,8},{10,11... | collective-permute-start | bytes 3932168 | tf_op jit(solution)/shard_map/ppermute | solution.py:12
  21.1 4.1 %copy-start.36 = (s32[1280]{0:T(1024)S(1)}, s32[1280]{0:T(1024)}, u32[]{:S(2)}) copy-start(s32[1280]{0:T(1024)} %param.18) | copy-start | bytes 15364
  25.3 3.8 %copy-start.7 = (bf16[1280,512]{1,0:T(8,128)(2,1)}, bf16[1280,512]{1,0:T(8,128)(2,1)S(1)}, u32[]{:S(2)}) copy-start(bf16[1280,512]{1,0:T(8,128)(2,1)S(1)} %gather_fusion.2) | copy-start | bytes 3932164
  33.2 2.4 copy-start.5
  33.2 2.4 copy-start.12
  43.6 3.2 copy-start.34
  46.8 13.6 %copy-start.16 = (bf16[160,512]{1,0:T(8,128)(2,1)S(1)}, bf16[160,512]{1,0:T(8,128)(2,1)}, u32[]{:S(2)}) copy-start(bf16[160,512]{1,0:T(8,128)(2,1)} %param.14) | copy-start | bytes 491524
  62.5 8.1 %copy-start.30 = (bf16[160,512]{1,0:T(8,128)(2,1)S(1)}, bf16[160,512]{1,0:T(8,128)(2,1)}, u32[]{:S(2)}) copy-start(bf16[160,512]{1,0:T(8,128)(2,1)} %param.16) | copy-start | bytes 491524
  62.5 8.1 %copy-start.38 = (f32[512]{0:T(512)S(1)}, f32[512]{0:T(512)}, u32[]{:S(2)}) copy-start(f32[512]{0:T(512)} %param.27) | copy-start | bytes 6148
  67.3 3.6 %copy-start.39 = (bf16[512,512]{1,0:T(8,128)(2,1)S(1)}, bf16[512,512]{1,0:T(8,128)(2,1)}, u32[]{:S(2)}) copy-start(bf16[512,512]{1,0:T(8,128)(2,1)} %param.26) | copy-start | bytes 1572868
  68.8 2.4 copy-start.32
  81.7 2.7 copy-start.2
  81.7 2.7 copy-start.4
  87.7 2.4 copy-start.9
  92.5 11.3 %copy-start.8 = (bf16[1280,512]{1,0:T(8,128)(2,1)S(1)}, bf16[1280,512]{1,0:T(8,128)(2,1)}, u32[]{:S(2)}) copy-start(bf16[1280,512]{1,0:T(8,128)(2,1)} %copy-done.7) | copy-start | bytes 3932164
  103.8 3.2 copy-start.21
  103.8 3.2 copy-start.31
  103.8 3.2 copy-start.33
  108.5 20.2 %all-to-all-start.1 = ((bf16[16,8,512]{2,1,0:T(8,128)(2,1)}), bf16[16,8,512]{2,1,0:T(8,128)(2,1)S(1)}, u32[]{:S(2)}, u32[]{:S(2)}) async-start(bf16[16,8,512]{2,1,0:T(8,128)(2,1)} %fusion.37), calls=%async_computation.2 | async-start | bytes 262144 | tf_op jit(solution)/shard_map/all_to_all | solution.py:167
  115.1 10.8 %copy-start.19 = (bf16[160,512]{1,0:T(8,128)(2,1)S(1)}, bf16[160,512]{1,0:T(8,128)(2,1)}, u32[]{:S(2)}) copy-start(bf16[160,512]{1,0:T(8,128)(2,1)} %copy-done.18) | copy-start | bytes 491524
  115.2 10.8 %copy-start.26 = (f32[160,512]{1,0:T(8,128)S(1)}, f32[160,512]{1,0:T(8,128)}, u32[]{:S(2)}) copy-start(f32[160,512]{1,0:T(8,128)} %reduce-scatter.3.cloned.1.call-done) | copy-start | bytes 983044
  115.2 12.2 %copy-start.17 = (bf16[160,512]{1,0:T(8,128)(2,1)S(1)}, bf16[160,512]{1,0:T(8,128)(2,1)}, u32[]{:S(2)}) copy-start(bf16[160,512]{1,0:T(8,128)(2,1)} %param.14) | copy-start | bytes 491524
  115.2 34.1 %reduce-scatter.5.cloned.1.call-start = ((), (), s32[]{:S(2)}) async-start(), calls=%async_computation.5 | async-start | bytes 983040 | tf_op jit(solution)/shard_map/reduce_scatter | solution.py:173
  131.2 3.3 %copy-start.6 = (bf16[1280,512]{1,0:T(8,128)(2,1)S(1)}, bf16[1280,512]{1,0:T(8,128)(2,1)}, u32[]{:S(2)}) copy-start(bf16[1280,512]{1,0:T(8,128)(2,1)} %copy-done.5) | copy-start | bytes 3932164
  131.2 3.3 %copy-start.10 = (bf16[1280,512]{1,0:T(8,128)(2,1)S(1)}, bf16[1280,512]{1,0:T(8,128)(2,1)}, u32[]{:S(2)}) copy-start(bf16[1280,512]{1,0:T(8,128)(2,1)} %copy-done.9) | copy-start | bytes 3932164
  131.2 183.9 %all-reduce.3.cloned.1.call-start = ((), (), s32[]{:S(2)}) async-start(), calls=%async_computation.6 | async-start | bytes 14680064 | tf_op jit(solution)/shard_map/psum | solution.py:179
  146.7 2.5 copy-start.14
  315.1 3.6 %copy-start.28 = (f32[512,512]{1,0:T(8,128)S(1)}, f32[512,512]{1,0:T(8,128)}, u32[]{:S(2)}) copy-start(f32[512,512]{1,0:T(8,128)} %get-tuple-element.23) | copy-start | bytes 3145732
  315.1 4.6 %copy-start.15 = (f32[1024,512]{1,0:T(8,128)S(1)}, f32[1024,512]{1,0:T(8,128)}, u32[]{:S(2)}) copy-start(f32[1024,512]{1,0:T(8,128)} %get-tuple-element.24) | copy-start | bytes 6291460
  (15 other events, 22.8 us)
Sparse Core Ops, SparseCore 0:
  58.1 9.1 reduce-scatter.2
  131.3 9.4 reduce-scatter.4
  147.0 168.1 all-reduce.2
where the time goes:
time: 330 us; the launch traced here: 328 us
  waiting for transfers between devices  169 us (51%)
  other arithmetic  53.9 us (16%)
  matrix products  40.7 us (12%)
  local copies, waits for them, and re-layouts  31 us (9%)
  starting transfers between devices  15.2 us (5%)
  between operations  14.3 us (4%)
  blocking collectives  4.59 us (1%)
    psum x1, waiting for transfers between devices, shards(): lax.psum((weight_grads[0], weight_grads[1], weight_grads[2], weight_grads...  164 us
    dot_general x7, matrix products, mat_mul(): return jnp.dot(left, right, preferred_element_type=jnp.float32)  16.4 us
    dot_general x7, matrix products, mat_tn(): lax.dot_general(left, right, (((0,), (0,)), ((), ())), preferred_element_...  12.4 us
    dot_general x7, matrix products, mat_nt(): lax.dot_general(left, right, (((1,), (1,)), ((), ())), preferred_element_...  11.9 us
    scatter-add x1, other arithmetic, shards(): jax.ops.segment_sum(message, receivers, num_segments=part_rows)  11.1 us
    scatter-add x1, other arithmetic, shards(): jax.ops.segment_sum(recv_grad, receivers, num_segments=part_rows)  10.7 us
    scatter-add x1, other arithmetic, shards(): jax.ops.segment_sum(send_grad, senders, num_segments=node_table.shape[0])  10.6 us
    unnamed x85, local copies, waits for them, and re-layouts  10.1 us
  transfers between devices with their start and end apart: 6, of which 2 were waited for; matrix products, arithmetic and copies ran while one was open for 15% of the time, Pallas kernels for 0%

commit v1 on v0

v1 whole, which is shorter than its diff:
```python
import functools
import math

import jax
import jax.numpy as jnp
from jax import lax
from jax.experimental import pallas as pl
from jax.experimental.pallas import tpu as pltpu
from jax.sharding import PartitionSpec as P

EPS = 1e-05
F32 = jnp.float32
BF16 = jnp.bfloat16
MESH = pl.DeviceIdType.MESH
VMEM = pltpu.VMEM


def swapped(array):
    return lax.ppermute(array, "rep", [(0, 1), (1, 0)])


def mat_mul(left, right):
    return jnp.dot(left, right, preferred_element_type=F32)


def mat_tn(left, right):
    return lax.dot_general(left, right, (((0,), (0,)), ((), ())), preferred_element_type=F32)


def mat_nt(left, right):
    return lax.dot_general(left, right, (((1,), (1,)), ((), ())), preferred_element_type=F32)


def sigmoid(value):
    return 1.0 / (1.0 + jnp.exp(-value))


def norm_forward(value):
    centred = value - jnp.mean(value, axis=-1, keepdims=True)
    inverse = lax.rsqrt(jnp.mean(centred * centred, axis=-1, keepdims=True) + EPS)
    return (centred * inverse, inverse)


def norm_backward(grad_hat, normed, inverse):
    return inverse * (
        grad_hat
        - jnp.mean(grad_hat, axis=-1, keepdims=True)
        - normed * jnp.mean(grad_hat * normed, axis=-1, keepdims=True)
    )


def picks(index, shape, axis):
    return jnp.where(lax.broadcasted_iota(jnp.int32, shape, axis) == index, 1.0, 0.0).astype(BF16)


def forward_kernel(
    edge, s_col, r_col, r_row, table, w_in, w_out, gain, offset,
    pre_out, normed_out, inv_out, totals, proj,
):
    width = edge.shape[1]
    tile = edge.shape[0]
    table_rows = table.shape[0]
    part_rows = totals.shape[0]

    @pl.when(pl.program_id(0) == 0)
    def _():
        totals[...] = jnp.zeros_like(totals)
        proj[:table_rows] = mat_mul(table[...], w_in[width : 2 * width]).astype(BF16)
        proj[table_rows:] = mat_mul(table[:part_rows], w_in[2 * width :]).astype(BF16)

    pre = (
        mat_mul(edge[...], w_in[:width])
        + mat_mul(picks(s_col[...], (tile, table_rows), 1), proj[:table_rows])
        + mat_mul(picks(r_col[...], (tile, part_rows), 1), proj[table_rows:])
    )
    pre_out[...] = pre
    hidden = (pre * sigmoid(pre)).astype(BF16)
    normed, inverse = norm_forward(mat_mul(hidden, w_out[...]))
    normed_out[...] = normed.astype(BF16)
    inv_out[...] = inverse
    message = (normed * gain[...] + offset[...]).astype(BF16)
    totals[...] += mat_mul(picks(r_row[...], (part_rows, tile), 0), message)


def node_kernel(
    scale, own, other, latent, cot, w_in, w_out, gain, totals_grad, base, w_grads
):
    width = latent.shape[1]
    half = latent.shape[0] // 2
    totals_b = (
        own[...] + jnp.concatenate([other[half:], other[:half]], 0)
    ).astype(BF16)
    rows = latent[...]
    pre = mat_mul(rows, w_in[:width]) + mat_mul(totals_b, w_in[width:])
    sig = sigmoid(pre)
    hidden = (pre * sig).astype(BF16)
    normed, inverse = norm_forward(mat_mul(hidden, w_out[...]))
    cots = cot[...].astype(F32)
    grad_out = norm_backward(cots * gain[...], normed, inverse).astype(BF16)
    grad_act = (mat_nt(grad_out, w_out[...]) * (sig * (1.0 + pre * (1.0 - sig)))).astype(BF16)
    totals_grad[...] = mat_nt(grad_act, w_in[width:]).astype(BF16)
    base[...] = mat_nt(grad_act[:half], w_in[:width]) + cots[:half]
    w_grads[:width] = (mat_tn(rows[:half], grad_act[:half]) * scale).astype(BF16)
    w_grads[width : 2 * width] = (mat_tn(totals_b[:half], grad_act[:half]) * scale).astype(BF16)
    w_grads[2 * width :] = (mat_tn(hidden[:half], grad_out[:half]) * scale).astype(BF16)


def backward_kernel(
    scale, edge, cot, pre_in, normed_in, inv_in, s_row, r_row, r_col,
    table, t_grad, w_in, w_out, gain, node_w,
    edge_grad, w_grads, row_grad, ghost_grad,
    acc_edge, acc_out, acc_send, acc_recv,
):
    width = edge.shape[1]
    tile = edge.shape[0]
    table_rows = table.shape[0]
    part_rows = t_grad.shape[0]

    @pl.when(pl.program_id(0) == 0)
    def _():
        acc_edge[...] = jnp.zeros_like(acc_edge)
        acc_out[...] = jnp.zeros_like(acc_out)
        acc_send[...] = jnp.zeros_like(acc_send)
        acc_recv[...] = jnp.zeros_like(acc_recv)

    cots = cot[...].astype(F32)
    message_grad = cots + mat_mul(picks(r_col[...], (tile, part_rows), 1), t_grad[...])
    grad_out = norm_backward(
        message_grad * gain[...], normed_in[...].astype(F32), inv_in[...]
    ).astype(BF16)
    pre = pre_in[...]
    sig = sigmoid(pre)
    hidden = (pre * sig).astype(BF16)
    grad_act = (mat_nt(grad_out, w_out[...]) * (sig * (1.0 + pre * (1.0 - sig)))).astype(BF16)
    edge_grad[...] = (cots + mat_nt(grad_act, w_in[:width])).astype(BF16)
    acc_edge[...] += mat_tn(edge[...], grad_act)
    acc_out[...] += mat_tn(hidden, grad_out)
    acc_send[...] += mat_mul(picks(s_row[...], (table_rows, tile), 0), grad_act)
    acc_recv[...] += mat_mul(picks(r_row[...], (part_rows, tile), 0), grad_act)

    @pl.when(pl.program_id(0) == pl.num_programs(0) - 1)
    def _():
        send = acc_send[...].astype(BF16)
        recv = acc_recv[...].astype(BF16)
        table_grad = mat_nt(send, w_in[width : 2 * width])
        row_grad[...] = table_grad[:part_rows] + mat_nt(recv, w_in[2 * width :])
        ghost_grad[...] = table_grad[part_rows:].astype(BF16)
        w_grads[:width] = (acc_edge[...] * scale).astype(BF16)
        w_grads[width : 2 * width] = (mat_tn(table[...], send) * scale).astype(BF16)
        w_grads[2 * width : 3 * width] = (mat_tn(table[:part_rows], recv) * scale).astype(BF16)
        w_grads[3 * width : 4 * width] = (acc_out[...] * scale).astype(BF16)
        w_grads[4 * width :] = node_w[...]


def orders(bits):
    return (
        tuple(range(bits)),
        tuple(b ^ 1 if (b ^ 1) < bits else b for b in range(bits)),
    )


def reduce_kernel(
    nodes, cuts, x, out, pair, acc, stage, landed,
    pair_sem, rs_sem, ag_sem, fw_sem,
):
    bits = nodes.bit_length() - 1
    me = lax.axis_index("nodes")
    rep = lax.axis_index("rep")
    other_rep = 1 - rep
    mine = [(me // (1 << b)) % 2 for b in range(bits)]
    flip = [(1 << b) * (1 - 2 * mine[b]) for b in range(bits)]
    streams = orders(bits)
    cols = [slice(*cut) for cut in cuts]

    def place(s, v):
        spot = me
        for k, b in enumerate(streams[s]):
            spot = spot + flip[b] * ((v // (1 << (bits - 1 - k))) % 2)
        return spot

    def partner(b):
        return {"nodes": me + flip[b]}

    barrier = pltpu.get_barrier_semaphore()
    for b in range(bits):
        pl.semaphore_signal(barrier, inc=1, device_id=partner(b), device_id_type=MESH)
    pl.semaphore_signal(barrier, inc=1, device_id={"rep": other_rep}, device_id_type=MESH)
    pl.semaphore_wait(barrier, bits + 1)

    first = []
    for s in range(2):
        copy = pltpu.make_async_remote_copy(
            src_ref=x.at[pl.ds(other_rep * nodes, nodes), :, cols[s]],
            dst_ref=pair.at[:, :, cols[s]],
            send_sem=pair_sem.at[0, s],
            recv_sem=pair_sem.at[1, s],
            device_id={"rep": other_rep},
            device_id_type=MESH,
        )
        copy.start()
        first.append(copy)

    def halve(s, k):
        half = nodes >> (k + 1)
        copy = pltpu.make_async_remote_copy(
            src_ref=stage.at[pl.ds(half, half), :, cols[s]],
            dst_ref=landed.at[pl.ds(half, half), :, cols[s]],
            send_sem=rs_sem.at[0, s, k],
            recv_sem=rs_sem.at[1, s, k],
            device_id=partner(streams[s][k]),
            device_id_type=MESH,
        )
        copy.start()
        return copy

    half = nodes // 2
    copies = {}
    for s in range(2):
        first[s].wait_recv()

        def load(v):
            spot = place(s, v)
            return x[rep * nodes + spot, :, cols[s]].astype(F32) + pair[spot, :, cols[s]].astype(F32)

        @pl.loop(half, nodes)
        def _(v):
            stage[v, :, cols[s]] = load(v).astype(BF16)

        copies[s, 0] = halve(s, 0)

    for s in range(2):

        def load(v):
            spot = place(s, v)
            return x[rep * nodes + spot, :, cols[s]].astype(F32) + pair[spot, :, cols[s]].astype(F32)

        @pl.loop(0, half)
        def _(v):
            acc[v, :, cols[s]] = load(v)

    for k in range(bits):
        half = nodes >> (k + 1)
        for s in range(2):
            copies[s, k].wait_recv()
            if k + 1 < bits:
                quarter = half // 2

                @pl.loop(quarter, half)
                def _(v):
                    stage[v, :, cols[s]] = (
                        acc[v, :, cols[s]] + landed[half + v, :, cols[s]].astype(F32)
                    ).astype(BF16)

                copies[s, k + 1] = halve(s, k + 1)

                @pl.loop(0, quarter)
                def _(v):
                    acc[v, :, cols[s]] = acc[v, :, cols[s]] + landed[half + v, :, cols[s]].astype(F32)
            else:
                out[rep * nodes + me, :, cols[s]] = (
                    acc[0, :, cols[s]] + landed[1, :, cols[s]].astype(F32)
                ).astype(BF16)

    def hand_on(s, v, sems, slot, device):
        spot = rep * nodes + place(s, v)
        copy = pltpu.make_async_remote_copy(
            src_ref=out.at[spot, :, cols[s]],
            dst_ref=out.at[spot, :, cols[s]],
            send_sem=sems.at[0, s, slot],
            recv_sem=sems.at[1, s, slot],
            device_id=device,
            device_id_type=MESH,
        )
        copy.start()
        return copy

    spread, forward = {}, {}
    for s in range(2):
        b = streams[s][bits - 1]
        spread[s, 1] = hand_on(s, 0, ag_sem, 1, partner(b))
        forward[s, 0] = hand_on(s, 0, fw_sem, 0, {"rep": other_rep})
    for k in range(bits - 1, -1, -1):
        half = nodes >> (k + 1)
        for s in range(2):
            for v in range(half, 2 * half):
                spot = rep * nodes + place(s, v)
                pltpu.make_async_remote_copy(
                    src_ref=out.at[spot, :, cols[s]],
                    dst_ref=out.at[spot, :, cols[s]],
                    send_sem=ag_sem.at[0, s, v],
                    recv_sem=ag_sem.at[1, s, v],
                    device_id=partner(streams[s][k]),
                    device_id_type=MESH,
                ).wait_recv()
            if k > 0:
                for v in range(2 * half):
                    slot = 2 * half + v
                    spread[s, slot] = hand_on(s, v, ag_sem, slot, partner(streams[s][k - 1]))
            for v in range(half, 2 * half):
                forward[s, v] = hand_on(s, v, fw_sem, v, {"rep": other_rep})
    for copy in forward.values():
        copy.wait_recv()
    for copy in [*first, *copies.values(), *spread.values(), *forward.values()]:
        copy.wait_send()


def reduced(x, nodes):
    count, rows, width = x.shape
    cuts = ((0, width // 2), (width // 2, width))
    bits = nodes.bit_length() - 1
    return pl.pallas_call(
        functools.partial(reduce_kernel, nodes, cuts),
        out_shape=jax.ShapeDtypeStruct(x.shape, BF16),
        in_specs=[pl.BlockSpec(memory_space=VMEM)],
        out_specs=pl.BlockSpec(memory_space=VMEM),
        scratch_shapes=[
            VMEM((nodes, rows, width), BF16),
            VMEM((nodes // 2, rows, width), F32),
            VMEM((nodes, rows, width), BF16),
            VMEM((nodes, rows, width), BF16),
            pltpu.SemaphoreType.DMA((2, 2)),
            pltpu.SemaphoreType.DMA((2, 2, bits)),
            pltpu.SemaphoreType.DMA((2, 2, nodes)),
            pltpu.SemaphoreType.DMA((2, 2, nodes)),
        ],
        compiler_params=pltpu.CompilerParams(collective_id=0, has_side_effects=True),
        name="weight_sum",
    )(x)


def whole():
    return pl.BlockSpec(memory_space=VMEM)


def shards(
    node_latent, edge_saved, node_cot, edge_cot, senders, receivers, ghost_rows,
    w_edge_in, w_edge_out, edge_gain, edge_offset, w_node_in, w_node_out, node_gain,
):
    width = node_latent.shape[1]
    own_rows = node_latent.shape[0]
    part_rows = 2 * own_rows
    edges = senders.shape[0]
    node_count = lax.axis_size("nodes")
    rep = lax.axis_index("rep")
    tile = 256
    tiles = edges // tile
    edge_scale = 1.0 / math.sqrt(edges * node_count * 2)
    node_scale = 1.0 / math.sqrt(own_rows * node_count * 2)

    def local(index):
        turned = (index + own_rows * rep) % part_rows
        return jnp.where(index < part_rows, turned, index)

    both = swapped(jnp.concatenate([node_latent, node_cot], 0))
    latent = jnp.concatenate([node_latent, both[:own_rows]], 0)
    cots = jnp.concatenate([node_cot, both[own_rows:]], 0)
    edge_latent = swapped(edge_saved)
    lists = local(ghost_rows[0])
    part_count, slots = lists.shape
    ghost_count = part_count * slots
    flat = lists.reshape(-1)
    outgoing = latent[flat].reshape(part_count, slots, width)
    ghosts = lax.all_to_all(outgoing, "nodes", split_axis=0, concat_axis=0, tiled=True)
    table = jnp.concatenate([latent, ghosts.reshape(ghost_count, width)], 0)
    table_rows = part_rows + ghost_count
    send = local(senders)
    recv = local(receivers)
    s_col, r_col = send[:, None], recv[:, None]
    s_row, r_row = send[None, :], recv[None, :]
    gain = edge_gain[None, :]

    edge_spec = pl.BlockSpec((tile, width), lambda i: (i, 0))
    col_spec = pl.BlockSpec((tile, 1), lambda i: (i, 0))
    row_spec = pl.BlockSpec((1, tile), lambda i: (0, i))
    params = pltpu.CompilerParams(dimension_semantics=("arbitrary",))

    pre, normed, inverse, partial_totals = pl.pallas_call(
        forward_kernel,
        grid=(tiles,),
        out_shape=(
            jax.ShapeDtypeStruct((edges, width), F32),
            jax.ShapeDtypeStruct((edges, width), BF16),
            jax.ShapeDtypeStruct((edges, 1), F32),
            jax.ShapeDtypeStruct((part_rows, width), F32),
        ),
        in_specs=[edge_spec, col_spec, col_spec, row_spec] + [whole()] * 5,
        out_specs=(edge_spec, edge_spec, col_spec, whole()),
        scratch_shapes=[VMEM((table_rows + part_rows, width), BF16)],
        compiler_params=params,
        name="edge_forward",
    )(edge_latent, s_col, r_col, r_row, table, w_edge_in, w_edge_out, gain, edge_offset[None, :])

    totals_grad, base, node_w = pl.pallas_call(
        functools.partial(node_kernel, node_scale),
        out_shape=(
            jax.ShapeDtypeStruct((part_rows, width), BF16),
            jax.ShapeDtypeStruct((own_rows, width), F32),
            jax.ShapeDtypeStruct((3 * width, width), BF16),
        ),
        in_specs=[whole()] * 7,
        out_specs=(whole(),) * 3,
        name="node_pass",
    )(
        partial_totals, swapped(partial_totals), latent, cots,
        w_node_in, w_node_out, node_gain[None, :],
    )

    edge_grad, w_grads, row_grad, ghost_grad = pl.pallas_call(
        functools.partial(backward_kernel, edge_scale),
        grid=(tiles,),
        out_shape=(
            jax.ShapeDtypeStruct((edges, width), BF16),
            jax.ShapeDtypeStruct((7 * width, width), BF16),
            jax.ShapeDtypeStruct((part_rows, width), F32),
            jax.ShapeDtypeStruct((ghost_count, width), BF16),
        ),
        in_specs=[edge_spec, edge_spec, edge_spec, edge_spec, col_spec, row_spec, row_spec, col_spec]
        + [whole()] * 6,
        out_specs=(edge_spec, whole(), whole(), whole()),
        scratch_shapes=[
            VMEM((width, width), F32),
            VMEM((width, width), F32),
            VMEM((table_rows, width), F32),
            VMEM((part_rows, width), F32),
        ],
        compiler_params=params,
        name="edge_backward",
    )(
        edge_latent, edge_cot, pre, normed, inverse, s_row, r_row, r_col,
        table, totals_grad, w_edge_in, w_edge_out, gain, node_w,
    )

    returned = lax.all_to_all(
        ghost_grad.reshape(part_count, slots, width), "nodes", split_axis=0, concat_axis=0, tiled=True
    ).reshape(ghost_count, width)
    taken = (lax.broadcasted_iota(jnp.int32, (part_rows, ghost_count), 0) == flat[None, :]).astype(BF16)
    row_grad = row_grad + mat_mul(taken, returned)
    grad_nodes = (row_grad[:own_rows] + swapped(row_grad[own_rows:]) + base).astype(BF16)

    devices = 2 * node_count
    total = reduced(w_grads.reshape(devices, 7 * width // devices, width), node_count)
    total = total.reshape(7 * width, width)
    return (
        grad_nodes,
        edge_grad,
        total[: 3 * width],
        total[3 * width : 4 * width],
        total[4 * width : 6 * width],
        total[6 * width :],
    )


def solution(mesh):
    return jax.shard_map(
        shards,
        mesh=mesh,
        in_specs=(
            P(("nodes", "rep"), None),
            P(("nodes", "rep"), None),
            P(("nodes", "rep"), None),
            P(("nodes", "rep"), None),
            P(("nodes", "rep")),
            P(("nodes", "rep")),
            P("nodes", None, None),
            P(),
            P(),
            P(),
            P(),
            P(),
            P(),
            P(),
        ),
        out_specs=(P(("nodes", "rep"), None), P(("nodes", "rep"), None), P(), P(), P(), P()),
        check_vma=False,
    )
```

time: 330 us -> 145 us (0.44)
  waiting for transfers between devices: 169 us -> 12.2 us
  Pallas kernels: 0 us -> 94.7 us
  other arithmetic: 53.9 us -> 5.49 us
  matrix products: 40.7 us -> 0.23 us
  local copies, waits for them, and re-layouts: 31 us -> 14.9 us
  between operations: 14.3 us -> 0.79 us
  blocking collectives: 4.59 us -> 0 us
    psum x1 -> x0, waiting for transfers between devices: 164 us -> none  [shards(): lax.psum((weight_grads[0], weight_grads[1], weight_grads[2], weight_grads...]
    pallas_call x0 -> x4, Pallas kernels: none -> 94.7 us  [the longest x1 64.5 us: reduced(): pl.pallas_call(functools.partial(reduce_kernel, nodes, cuts), out_shape=j...]
    dot_general x21 -> x1, matrix products: 40.7 us -> 0.23 us  [mat_mul(): return jnp.dot(left, right, preferred_element_type=F32)]
    scatter-add x4 -> x0, other arithmetic: 33.9 us -> none  [the longest x1 11.1 us: shards(): jax.ops.segment_sum(message, receivers, num_segments=part_rows)]
    gather x5 -> x1, local copies, waits for them, and re-layouts: 16.8 us -> 1.5 us  [shards(): outgoing = latent[flat].reshape(part_count, slots, width)]
    unnamed x85 -> x17, local copies, waits for them, and re-layouts: 10.1 us -> 2.67 us
    slice x1 -> x5, local copies, waits for them, and re-layouts: 0.04 us -> 7.24 us  [the longest x1 2.65 us: shards(): total[:3 * width]]
    convert_element_type x5 -> x1, other arithmetic: 7.72 us -> 0.73 us  [shards(): (row_grad[:own_rows] + swapped(row_grad[own_rows:]) + base).astype(BF16)]
  transfers between devices with their start and end apart: 6 -> 6, of which waited for: 2 -> 4; matrix products, arithmetic and copies ran while one was open for 15% -> 12% of each run, Pallas kernels for 0% -> 45%
where the time goes in v1:
time: 145 us; the launch traced here: 144 us
  Pallas kernels  94.7 us (65%)
  starting transfers between devices  15.6 us (11%)
  local copies, waits for them, and re-layouts  14.9 us (10%)
  waiting for transfers between devices  12.2 us (8%)
  other arithmetic  5.49 us (4%)
    pallas_call x1, Pallas kernels, reduced(): pl.pallas_call(functools.partial(reduce_kernel, nodes, cuts), out_shape=j...  64.5 us
    pallas_call x1, Pallas kernels, shards(): pl.pallas_call(functools.partial(backward_kernel, edge_scale), grid=(tile...  14.6 us
    pallas_call x1, Pallas kernels, shards(): pl.pallas_call(forward_kernel, grid=(tiles,), out_shape=(jax.ShapeDtypeSt...  10.3 us
    all_to_all x1, starting transfers between devices, shards(): lax.all_to_all(outgoing, 'nodes', split_axis=0, concat_axis=0, tiled=True)  7.7 us
    all_to_all x1, waiting for transfers between devices, shards(): lax.all_to_all(ghost_grad.reshape(part_count, slots, width), 'nodes', spl...  6.51 us
    pallas_call x1, Pallas kernels, shards(): pl.pallas_call(functools.partial(node_kernel, node_scale), out_shape=(jax...  5.31 us
    ppermute x4, starting transfers between devices, swapped(): return lax.ppermute(array, 'rep', [(0, 1), (1, 0)])  4.34 us
    all_to_all x1, waiting for transfers between devices, shards(): lax.all_to_all(outgoing, 'nodes', split_axis=0, concat_axis=0, tiled=True)  3.85 us
  transfers between devices with their start and end apart: 6, of which 4 were waited for; matrix products, arithmetic and copies ran while one was open for 12% of the time, Pallas kernels for 45%

profile of v1, /device:TPU:1, one launch (start us, length us, event | category | flops | bytes accessed | tf_op | source)
XLA Modules:
  0.0 143.9 jit_solution(12425531151224209447)
XLA Ops:
  0.7 1.0 pad_maximum_fusion.2
  1.8 0.6 collective-permute-start.1
  2.3 0.8 copy.22
  3.1 0.1 squeeze.5
  3.2 1.2 collective-permute-done.1
  4.5 0.9 pad_maximum_fusion.1.latent
  5.4 1.5 %gather_fusion = bf16[128,512]{1,0:T(8,128)(2,1)} fusion(bf16[320,512]{1,0:T(8,128)(2,1)S(1)} %pad_maximum_fusion.1.latent, s32[1024]{0:T(1024)S(1)} %pad_clamp_fusion), kind=kCustom, calls=%fused_computation | custom fusion | bytes 262656 | tf_op jit(solution)/shard_map/gather | solution.py:362
  6.9 7.7 %all-to-all-start = ((bf16[16,8,512]{2,1,0:T(8,128)(2,1)}), bf16[16,8,512]{2,1,0:T(8,128)(2,1)S(1)}, u32[]{:S(2)}, u32[]{:S(2)}) async-start(bf16[16,8,512]{2,1,0:T(8,128)(2,1)} %bitcast.1), calls=%async_computation | async-start | bytes 262144 | tf_op jit(solution)/shard_map/all_to_all | solution.py:363
  14.7 0.6 broadcast_in_dim.24.r_row
  15.3 1.1 broadcast_in_dim.30.r_col
  16.4 1.1 broadcast_in_dim.29.s_col
  17.4 3.9 %all-to-all-done = bf16[16,8,512]{2,1,0:T(8,128)(2,1)S(1)} async-done(((bf16[16,8,512]{2,1,0:T(8,128)(2,1)}), bf16[16,8,512]{2,1,0:T(8,128)(2,1)S(1)}, u32[]{:S(2)}, u32[]{:S(2)}) %all-to-all-start) | async-done | bytes 131104 | tf_op jit(solution)/shard_map/all_to_all | solution.py:363
  21.3 0.8 pad_maximum_fusion.table
  22.1 1.1 copy-done.1
  23.2 10.3 %edge_forward.1 = (f32[1280,512]{1,0:T(8,128)}, bf16[1280,512]{1,0:T(8,128)(2,1)}, f32[1280,1]{1,0:T(8,128)}, f32[320,512]{1,0:T(8,128)}) custom-call(bf16[1280,512]{1,0:T(8,128)(2,1)} %copy-done.1, s32[1280,1]{1,0:T(8,128)} %broadcast_in_dim.29.s_col, s32[1280,1]{1,0:T(8,128)} %broadcast_in_dim.30.r_col, s32[1,1280]{1,0:T(1,128)} %broadcast_in_dim.24.r_row, ...), custom_call_target="tpu_custom_call" | custom-call | tf_op jit(solution)/shard_map/edge_forward/pallas_call | solution.py:377
  33.5 1.9 %collective-permute-start.2 = (f32[320,512]{1,0:T(8,128)}, f32[320,512]{1,0:T(8,128)S(1)}, u32[]{:S(2)}, u32[]{:S(2)}) collective-permute-start(f32[320,512]{1,0:T(8,128)} %get-tuple-element.20.own), channel_id=1, source_target_pairs={{0,1},{1,0},{2,3},{3,2},{4,5},{5,4},{6,7},{7,6},{8,9},{9,8},{10,11... | collective-permute-start | bytes 1966088 | tf_op jit(solution)/shard_map/ppermute | solution.py:19
  35.4 0.6 broadcast_in_dim.27.s_row
  36.0 0.8 pad_maximum_fusion.3.cot
  36.7 0.6 collective-permute-done.2.other
  37.3 0.8 copy-done.4
  38.1 5.3 %node_pass.1 = (bf16[320,512]{1,0:T(8,128)(2,1)}, f32[160,512]{1,0:T(8,128)}, bf16[1536,512]{1,0:T(8,128)(2,1)}) custom-call(f32[320,512]{1,0:T(8,128)} %get-tuple-element.20.own, f32[320,512]{1,0:T(8,128)} %copy-done.4, bf16[320,512]{1,0:T(8,128)(2,1)} %copy-done, bf16[320,512]{1,0:T(8,128)(2,1)} %pad_maximum_fusion.3.cot, bf16[1024,512]{1,0:T(8,128)(2,1)} %w_in.4, ...), custom_call_target="tpu_custom_call" | custom-call | tf_op jit(solution)/shard_map/node_pass/pallas_call | solution.py:393
  43.4 14.6 %edge_backward.1 = (bf16[1280,512]{1,0:T(8,128)(2,1)}, bf16[3584,512]{1,0:T(8,128)(2,1)}, f32[320,512]{1,0:T(8,128)}, bf16[128,512]{1,0:T(8,128)(2,1)}) custom-call(bf16[1280,512]{1,0:T(8,128)(2,1)} %copy-done.1, bf16[1280,512]{1,0:T(8,128)(2,1)} %cot.1, f32[1280,512]{1,0:T(8,128)} %get-tuple-element.17.pre_in, ...), custom_call_target="tpu_custom_call" | custom-call | tf_op jit(solution)/shard_map/edge_backward/pallas_call | solution.py:408
  58.1 3.5 %all-to-all-start.1 = ((bf16[16,8,512]{2,1,0:T(8,128)(2,1)}), bf16[16,8,512]{2,1,0:T(8,128)(2,1)S(1)}, u32[]{:S(2)}, u32[]{:S(2)}) async-start(bf16[16,8,512]{2,1,0:T(8,128)(2,1)} %bitcast.18), calls=%async_computation.1 | async-start | bytes 262144 | tf_op jit(solution)/shard_map/all_to_all | solution.py:433
  61.7 6.5 %all-to-all-done.1 = bf16[16,8,512]{2,1,0:T(8,128)(2,1)S(1)} async-done(((bf16[16,8,512]{2,1,0:T(8,128)(2,1)}), bf16[16,8,512]{2,1,0:T(8,128)(2,1)S(1)}, u32[]{:S(2)}, u32[]{:S(2)}) %all-to-all-start.1) | async-done | bytes 131104 | tf_op jit(solution)/shard_map/all_to_all | solution.py:433
  68.2 0.2 fusion.2
  68.4 1.2 add.94
  69.7 1.8 %collective-permute-start.3 = (f32[160,512]{1,0:T(8,128)S(1)}, f32[160,512]{1,0:T(8,128)S(1)}, u32[]{:S(2)}, u32[]{:S(2)}) collective-permute-start(f32[160,512]{1,0:T(8,128)S(1)} %slice.37), channel_id=1, source_target_pairs={{0,1},{1,0},{2,3},{3,2},{4,5},{5,4},{6,7},{7,6},{8,9},{9,8},{10,11... | collective-permute-start | bytes 983048 | tf_op jit(solution)/shard_map/ppermute | solution.py:19
  71.5 64.5 %weight_sum.1 = bf16[32,112,512]{2,1,0:T(8,128)(2,1)} custom-call(bf16[32,112,512]{2,1,0:T(8,128)(2,1)} %bitcast.16), custom_call_target="tpu_custom_call" | custom-call | tf_op jit(solution)/shard_map/weight_sum/pallas_call | solution.py:311
  136.0 2.3 %slice.40 = bf16[1024,512]{1,0:T(8,128)(2,1)} slice(bf16[3584,512]{1,0:T(8,128)(2,1)} %bitcast.13), slice={[2048:3072], [0:512]} | slice | bytes 2097152 | tf_op jit(solution)/shard_map/slice | solution.py:448
  138.2 2.7 %slice.38 = bf16[1536,512]{1,0:T(8,128)(2,1)} slice(bf16[3584,512]{1,0:T(8,128)(2,1)} %bitcast.14), slice={[0:1536], [0:512]} | slice | bytes 3145728 | tf_op jit(solution)/shard_map/slice | solution.py:446
  140.9 2.3 %fusion.12 = (bf16[512,512]{1,0:T(8,128)(2,1)}, bf16[512,512]{1,0:T(8,128)(2,1)}) fusion(bf16[3584,512]{1,0:T(8,128)(2,1)} %bitcast.15), kind=kLoop, calls=%fused_computation.31 | loop fusion | bytes 2097152 | tf_op jit(solution)/shard_map/slice | solution.py:449
  143.2 0.7 fusion.1
  (24 shorter events, 0.3 us)
Async XLA Ops:
  0.6 14.0 %copy-start.6 = (s32[1280]{0:T(1024)S(1)}, s32[1280]{0:T(1024)}, u32[]{:S(2)}) copy-start(s32[1280]{0:T(1024)} %param.19) | copy-start | bytes 15364
  0.6 14.0 %copy-start.7 = (s32[1280]{0:T(1024)S(1)}, s32[1280]{0:T(1024)}, u32[]{:S(2)}) copy-start(s32[1280]{0:T(1024)} %param.18) | copy-start | bytes 15364
  0.7 21.4 %collective-permute-start = (bf16[1280,512]{1,0:T(8,128)(2,1)}, bf16[1280,512]{1,0:T(8,128)(2,1)S(1)}, u32[]{:S(2)}, u32[]{:S(2)}) collective-permute-start(bf16[1280,512]{1,0:T(8,128)(2,1)} %param.15), channel_id=1, source_target_pairs={{0,1},{1,0},{2,3},{3,2},{4,5},{5,4},{6,7},{7,6},{8,9},{9,8},{10,11... | collective-permute-start | bytes 3932168 | tf_op jit(solution)/shard_map/ppermute | solution.py:19
  1.8 2.7 %collective-permute-start.1 = (bf16[320,512]{1,0:T(8,128)(2,1)S(1)}, bf16[320,512]{1,0:T(8,128)(2,1)S(1)}, u32[]{:S(2)}, u32[]{:S(2)}) collective-permute-start(bf16[320,512]{1,0:T(8,128)(2,1)S(1)} %pad_maximum_fusion.2), channel_id=1, source_target_pairs={{0,1},{1,0},{2,3},{3,2},{4,5},{5,4},{6,7},{7,6},{8,9},{9,8},{10,11... | collective-permute-start | bytes 983048 | tf_op jit(solution)/shard_map/ppermute | solution.py:19
  5.4 16.7 %copy-start = (bf16[320,512]{1,0:T(8,128)(2,1)}, bf16[320,512]{1,0:T(8,128)(2,1)S(1)}, u32[]{:S(2)}) copy-start(bf16[320,512]{1,0:T(8,128)(2,1)S(1)} %pad_maximum_fusion.1.latent) | copy-start | bytes 983044
  5.4 15.9 %copy-start.2 = (bf16[160,512]{1,0:T(8,128)(2,1)S(1)}, bf16[160,512]{1,0:T(8,128)(2,1)}, u32[]{:S(2)}) copy-start(bf16[160,512]{1,0:T(8,128)(2,1)} %param.14) | copy-start | bytes 491524
  6.9 14.4 %all-to-all-start = ((bf16[16,8,512]{2,1,0:T(8,128)(2,1)}), bf16[16,8,512]{2,1,0:T(8,128)(2,1)S(1)}, u32[]{:S(2)}, u32[]{:S(2)}) async-start(bf16[16,8,512]{2,1,0:T(8,128)(2,1)} %bitcast.1), calls=%async_computation | async-start | bytes 262144 | tf_op jit(solution)/shard_map/all_to_all | solution.py:363
  22.1 1.1 copy-start.1
  23.2 12.8 %copy-start.3 = (bf16[160,512]{1,0:T(8,128)(2,1)S(1)}, bf16[160,512]{1,0:T(8,128)(2,1)}, u32[]{:S(2)}) copy-start(bf16[160,512]{1,0:T(8,128)(2,1)} %param.16) | copy-start | bytes 491524
  33.5 3.8 %collective-permute-start.2 = (f32[320,512]{1,0:T(8,128)}, f32[320,512]{1,0:T(8,128)S(1)}, u32[]{:S(2)}, u32[]{:S(2)}) collective-permute-start(f32[320,512]{1,0:T(8,128)} %get-tuple-element.20.own), channel_id=1, source_target_pairs={{0,1},{1,0},{2,3},{3,2},{4,5},{5,4},{6,7},{7,6},{8,9},{9,8},{10,11... | collective-permute-start | bytes 1966088 | tf_op jit(solution)/shard_map/ppermute | solution.py:19
  37.3 0.8 copy-start.4
  58.1 10.1 %all-to-all-start.1 = ((bf16[16,8,512]{2,1,0:T(8,128)(2,1)}), bf16[16,8,512]{2,1,0:T(8,128)(2,1)S(1)}, u32[]{:S(2)}, u32[]{:S(2)}) async-start(bf16[16,8,512]{2,1,0:T(8,128)(2,1)} %bitcast.18), calls=%async_computation.1 | async-start | bytes 262144 | tf_op jit(solution)/shard_map/all_to_all | solution.py:433
  69.7 73.5 %collective-permute-start.3 = (f32[160,512]{1,0:T(8,128)S(1)}, f32[160,512]{1,0:T(8,128)S(1)}, u32[]{:S(2)}, u32[]{:S(2)}) collective-permute-start(f32[160,512]{1,0:T(8,128)S(1)} %slice.37), channel_id=1, source_target_pairs={{0,1},{1,0},{2,3},{3,2},{4,5},{5,4},{6,7},{7,6},{8,9},{9,8},{10,11... | collective-permute-start | bytes 983048 | tf_op jit(solution)/shard_map/ppermute | solution.py:19
  140.9 2.3 %copy-start.5 = (f32[160,512]{1,0:T(8,128)S(1)}, f32[160,512]{1,0:T(8,128)}, u32[]{:S(2)}) copy-start(f32[160,512]{1,0:T(8,128)} %get-tuple-element.25) | copy-start | bytes 983044
